TPU v7x, 32 devices: a whole 2x2x4 slice. The times are simulated.
32 devices in a mesh: pp: 4 (over y, x), cp: 4 (over z), tp: 2 (over core).
Axes of the slice: x: 2, y: 2, z: 4, core: 2. Of those that a mesh axis runs over, the one named last changes fastest.
Arguments:
- queries: bfloat16 [2048, 16384], P(('pp', 'cp'), 'tp'), may hold values from -12 to 12
- keys: bfloat16 [2048, 1024], P(('pp', 'cp'), 'tp'), may hold values from -12 to 12
- values: bfloat16 [2048, 1024], P(('pp', 'cp'), 'tp'), may hold values from -6 to 6
- pair_order: int32 [4, 4], replicated, may hold values from 0 to 3, each once within a row
- lengths: int32 [4, 2], replicated, may hold values from 128 to 256
- routes: int32 [4, 512, 1], P(None, 'cp'), may hold values from 0 to 7; in each aligned block of 128 rows (0 to 127, 128 to 255, ..., all dimensions but the last counted through in order) at most 32 rows name the same one
Outputs:
- rebalanced: bfloat16 [4096, 16384], P(('pp', 'cp', 'tp'))
Inputs may be any that keep to these rules, and one draw needn't show every extreme that they name: `routes`: at most 32 rows of one device's block name the same destination, and in some block one destination is named by exactly 32 rows.
All inputs are finite; a program needn't handle non-finite values.
Results may differ from a plain program's by a relative error of at most 0.003.
Values may be sent and summed in bfloat16 or wider, within the bound.
No kernel may reach another device: no remote copies, remote signals or barrier semaphores. Data moves between devices by JAX's collectives and lax.ppermute only.
A program may use at most 64 MiB of HBM per device.

v0:
```python
import jax
import jax.numpy as jnp
from jax import lax
from jax.sharding import PartitionSpec as P

HD = 128
masked_score = -1e30


def shifted(block, axis, distance):
    devices = range(lax.axis_size(axis))
    route = [((i - distance) % len(devices), i) for i in devices]
    return lax.ppermute(block, axis, route)


def pair_positions(pair_ids, block_len, cycle_size):
    offsets = jnp.arange(block_len, dtype=jnp.int32)
    first_half = pair_ids[:, None] * block_len + offsets[None, :]
    second_half = (2 * cycle_size - 1 - pair_ids)[:, None] * block_len + offsets[None, :]
    return jnp.concatenate([first_half, second_half], axis=1)


def dispatch_rows(attended, targets, dest_count, capacity):
    row_count = attended.shape[0]
    matches = targets[:, None] == jnp.arange(dest_count, dtype=jnp.int32)[None, :]
    row_ids = jnp.arange(row_count, dtype=jnp.int32)
    earlier = (row_ids[None, :] < row_ids[:, None]).astype(jnp.bfloat16)
    before = jnp.dot(earlier, matches.astype(jnp.bfloat16), preferred_element_type=jnp.float32)
    slot_index = jnp.sum(jnp.where(matches, before, 0.0), axis=1).astype(jnp.int32)
    slot_ids = jnp.arange(capacity, dtype=jnp.int32)
    picked_rows = jnp.logical_and(
        jnp.transpose(matches)[:, None, :], slot_index[None, None, :] == slot_ids[None, :, None]
    )
    selector = picked_rows.astype(jnp.bfloat16).reshape(dest_count * capacity, row_count)
    return jnp.dot(selector, attended, preferred_element_type=jnp.float32).astype(jnp.bfloat16)


def spread_rows(buffer, cycle_size, split_size, capacity, width):
    flat_buffer = buffer.reshape(cycle_size * split_size, capacity, width)
    moved = lax.all_to_all(flat_buffer, ("cp", "tp"), split_axis=0, concat_axis=0, tiled=True)
    moved = jnp.transpose(moved.reshape(cycle_size, split_size, capacity, width), (0, 2, 1, 3))
    return moved.reshape(cycle_size * capacity, split_size * width)


def arrange_rows(attended, routes, source, cycle_size, split_size):
    row_count, width = attended.shape
    dest_count = cycle_size * split_size
    capacity = 2 * row_count // dest_count
    targets = lax.dynamic_index_in_dim(routes, source, 0, keepdims=False)[:, 0]
    buffer = dispatch_rows(attended, targets, dest_count, capacity)
    buffer = buffer.reshape(cycle_size, split_size, capacity, width)
    return spread_rows(buffer, cycle_size, split_size, capacity, width)


def body(queries, keys, values, pair_order, lengths, routes):
    cycle_size = lax.axis_size("cp")
    split_size = lax.axis_size("tp")
    section = lax.axis_index("pp")
    place = lax.axis_index("cp")
    row_count = queries.shape[0]
    block_len = row_count // 4
    width = queries.shape[1]
    group_count = keys.shape[1] // HD
    group_size = width // keys.shape[1]
    score_scale = HD ** (-0.5)
    order_row = lax.dynamic_index_in_dim(pair_order, section, 0, keepdims=False)
    own_pair = lax.dynamic_index_in_dim(order_row, place, 0, keepdims=True)
    query_pos = pair_positions(own_pair, block_len, cycle_size).reshape(2 * block_len)
    limits = lax.dynamic_index_in_dim(lengths, section, 0, keepdims=False)
    query_rows = queries.reshape(2, 2 * block_len, group_count, group_size, HD)
    stat_shape = (2, 2 * block_len, group_count, group_size)
    start_state = (
        jnp.full(stat_shape, masked_score, jnp.float32),
        jnp.zeros(stat_shape, jnp.float32),
        jnp.zeros(stat_shape + (HD,), jnp.float32),
    )
    state = start_state
    key_piece = lax.all_gather(keys, "cp", axis=0, tiled=True)
    value_piece = lax.all_gather(values, "cp", axis=0, tiled=True)
    shard_count = key_piece.shape[0] // row_count
    first_shard = jnp.int32(0) // row_count
    for base in range(0, shard_count, 4):
        block = min(4, shard_count - base)
        key_block = key_piece[base * row_count : (base + block) * row_count].reshape(
            block, 2, 2 * block_len, group_count, HD
        )
        value_block = value_piece[base * row_count : (base + block) * row_count].reshape(
            block, 2, 2 * block_len, group_count, HD
        )
        shard_ids = first_shard + base + jnp.arange(block, dtype=jnp.int32)
        key_pos = pair_positions(order_row[shard_ids], block_len, cycle_size).reshape(
            block * 2 * block_len
        )
        allowed = jnp.logical_and(
            key_pos[None, None, :] <= query_pos[None, :, None],
            key_pos[None, None, :] < limits[:, None, None],
        )
        allowed = allowed[:, :, None, None, :]
        scores = jnp.einsum(
            "sqgrd,nskgd->sqgrnk", query_rows, key_block, preferred_element_type=jnp.float32
        )
        scores = scores.reshape(stat_shape + (block * 2 * block_len,)) * score_scale
        running_max, running_total, running_sum = state
        block_max = jnp.max(jnp.where(allowed, scores, masked_score), axis=4)
        new_max = jnp.maximum(running_max, block_max)
        weights = jnp.where(allowed, jnp.exp(scores - new_max[..., None]), 0.0)
        carry_factor = jnp.exp(running_max - new_max)
        running_total = running_total * carry_factor + jnp.sum(weights, axis=4)
        shaped = weights.astype(jnp.bfloat16).reshape(stat_shape + (block, 2 * block_len))
        running_sum = running_sum * carry_factor[..., None] + jnp.einsum(
            "sqgrnk,nskgd->sqgrd", shaped, value_block, preferred_element_type=jnp.float32
        )
        state = (new_max, running_total, running_sum)
    attended = (state[2] / state[1][..., None]).astype(jnp.bfloat16).reshape(row_count, width)
    arranged = arrange_rows(attended, routes, section, cycle_size, split_size)
    return shifted(arranged, "pp", 1)


def solution(mesh):
    placed = (
        P(("pp", "cp"), "tp"),
        P(("pp", "cp"), "tp"),
        P(("pp", "cp"), "tp"),
        P(),
        P(),
        P(None, "cp", None),
    )
    return jax.shard_map(
        body, mesh=mesh, in_specs=placed, out_specs=P(("pp", "cp", "tp"), None), check_vma=False
    )
```

profile of v0, /device:TPU:0, one launch (start us, length us, event | category | flops | bytes accessed | tf_op | source)
XLA Modules:
  0.0 287.3 jit_solution(959507155664328261)
XLA Ops:
  0.0 0.0 copy-start
  0.0 0.0 copy-start.2
  0.0 0.7 copy-done
  0.7 0.1 fusion.9
  0.9 0.7 fusion.14
  1.6 1.3 dynamic_slice.18
  4.1 0.6 gather_fusion
  4.8 0.9 dynamic-slice_reduce_fusion
  5.7 0.1 add_bitcast_fusion
  5.7 0.1 iota_add_fusion
  5.8 0.1 pad_add_fusion
  5.9 0.1 broadcast_compare_fusion
  6.0 0.1 broadcast_compare_fusion.1
  6.1 2.2 copy.30
  8.3 0.0 copy-done.2
  8.3 17.4 %all_gather.6 = bf16[512,512]{1,0:T(8,128)(2,1)S(1)} all-gather(bf16[128,512]{1,0:T(8,128)(2,1)S(1)} %copy-done.2), channel_id=1, replica_groups=mesh['pp'=4,'cp'=4,'tp'=2] {'cp'}, dimensions={0}, use_global_device_ids=true | all-gather | bytes 655360 | tf_op jit(solution)/shard_map/all_gather | solution.py:78
  25.6 0.1 reshape.234
  25.8 0.1 broadcast_and_fusion
  25.9 5.5 %fusion = (f32[2,64,4,16]{1,3,2,0:T(8,128)S(1)}, f32[2,4,4,64,64,16]{4,3,5,2,1,0:T(8,128)S(1)}) fusion(pred[2,64,4,64]{1,3,2,0:T(8,128)(4,1)S(1)} %broadcast_and_fusion, bf16[2,64,4,16,128,1]{4,3,2,1,0,5:T(8,128)(2,1)S(1)} %bitcast.52, bf16[4,2,64,4,128,1]{4,3,2,1,0,5:T(4,128)(2,1)S(1)} %bitcast.54), kind=kOutput, calls=%fused_computation.3 | convolution fusion | flops 543154176 | bytes 11075584 | tf_op jit(solution)/shard_map/sqgrd,nskgd->sqgrnk/dot_general | solution.py:99
  31.4 6.2 %fusion.3 = (f32[2,64,4,16]{1,3,2,0:T(8,128)S(1)}, bf16[2,64,4,16,4,64]{1,5,3,4,2,0:T(8,128)(2,1)}) fusion(f32[2,4,4,64,64,16]{4,3,5,2,1,0:T(8,128)S(1)} %get-tuple-element.12, f32[2,64,4,16]{1,3,2,0:T(8,128)S(1)} %broadcast_maximum_fusion, pred[2,64,4,64]{1,3,2,0:T(8,128)(4,1)S(1)} %broadcast_and_fusion), kind=kLoop, calls=%fused_computation.6 | loop fusion | flops 10477568 | bytes 12681216 | tf_op jit(solution)/shard_map/reduce_sum | solution.py:108
  37.7 0.1 copy.14
  37.8 0.1 copy.17
  38.0 0.0 copy-start.3
  38.0 17.2 %copy.15 = bf16[2,64,4,16,4,64]{5,3,4,1,2,0:T(8,128)(2,1)} copy(bf16[2,64,4,16,4,64]{1,5,3,4,2,0:T(8,128)(2,1)} %get-tuple-element.6) | data formatting | bytes 8388608 | tf_op jit(solution)/shard_map/convert_element_type | solution.py:109
  55.2 0.0 copy-done.3
  55.2 16.2 %all_gather.7 = bf16[512,512]{1,0:T(8,128)(2,1)S(1)} all-gather(bf16[128,512]{1,0:T(8,128)(2,1)S(1)} %copy-done.3), channel_id=1, replica_groups=mesh['pp'=4,'cp'=4,'tp'=2] {'cp'}, dimensions={0}, use_global_device_ids=true | all-gather | bytes 655360 | tf_op jit(solution)/shard_map/all_gather | solution.py:79
  71.4 0.1 reshape.236
  71.6 5.7 %fusion.6 = bf16[2,64,4,16,128]{4,3,1,2,0:T(8,128)(2,1)S(1)} fusion(bf16[2,64,4,16,4,64]{5,3,4,1,2,0:T(8,128)(2,1)} %copy.15, f32[2,64,4,16]{3,1,2,0:T(8,128)S(1)} %copy.17, f32[2,64,4,16]{3,1,2,0:T(8,128)S(1)} %copy.14, bf16[4,2,64,4,128,1]{4,3,2,1,0,5:T(4,128)(2,1)S(1)} %bitcast.56), kind=kOutput, calls=%fused_computation.11 | convolution fusion | flops 540016640 | bytes 6881280 | tf_op jit(solution)/shard_map/sqgrnk,nskgd->sqgrd/dot_general | solution.py:110
  77.3 1.9 copy.18
  79.2 2.8 reshape.237
  82.1 1.2 convolution_convert_fusion
  83.3 97.9 %all_to_all.5 = bf16[8,32,8192]{2,1,0:T(8,128)(2,1)S(1)} all-to-all(bf16[8,32,8192]{2,1,0:T(8,128)(2,1)S(1)} %bitcast.49), channel_id=1, replica_groups=mesh['pp'=4,'cp'=4,'tp'=2] {'cp','tp'}, dimensions={0} | all-to-all | bytes 8388608 | tf_op jit(solution)/shard_map/all_to_all | solution.py:40
  181.2 6.4 %copy.19 = bf16[4,2,32,8192]{3,1,2,0:T(2,128)(2,1)} copy(bf16[4,2,32,8192]{3,2,1,0:T(8,128)(2,1)S(1)} %bitcast.50) | data formatting | bytes 8388608 | tf_op jit(solution)/shard_map/reshape | solution.py:41
  187.6 4.8 %copy.31 = bf16[16,8,2,8192]{3,1,2,0:T(8,128)(2,1)S(1)} copy(bf16[16,8,2,8192]{3,2,1,0:T(2,128)(2,1)} %bitcast.51) | data formatting | bytes 8388608
  192.4 0.0 copy-start.1
  192.4 1.6 collective-permute-start
  194.0 91.3 %collective-permute-done = bf16[128,16384]{1,0:T(8,128)(2,1)S(1)} collective-permute-done((bf16[128,16384]{1,0:T(8,128)(2,1)S(1)}, bf16[128,16384]{1,0:T(8,128)(2,1)S(1)}, u32[]{:S(2)}, u32[]{:S(2)}) %collective-permute-start) | collective-permute-done | bytes 4194336 | tf_op jit(solution)/shard_map/ppermute | solution.py:13
  285.3 2.0 copy.45
  287.3 0.0 copy-done.1
  (11 shorter events, 0.1 us)
Async XLA Ops:
  0.0 0.7 copy-start
  0.0 8.3 %copy-start.2 = (bf16[128,512]{1,0:T(8,128)(2,1)S(1)}, bf16[128,512]{1,0:T(8,128)(2,1)}, u32[]{:S(2)}) copy-start(bf16[128,512]{1,0:T(8,128)(2,1)} %param.7) | copy-start | bytes 393220
  38.0 17.2 %copy-start.3 = (bf16[128,512]{1,0:T(8,128)(2,1)S(1)}, bf16[128,512]{1,0:T(8,128)(2,1)}, u32[]{:S(2)}) copy-start(bf16[128,512]{1,0:T(8,128)(2,1)} %param.8) | copy-start | bytes 393220
  192.4 94.9 %copy-start.1 = (s32[4,128,1]{1,2,0:T(1,128)S(1)}, s32[4,128,1]{1,2,0:T(1,128)}, u32[]{:S(2)}) copy-start(s32[4,128,1]{1,2,0:T(1,128)} %param.11) | copy-start | bytes 6148
  192.4 92.9 %collective-permute-start = (bf16[128,16384]{1,0:T(8,128)(2,1)S(1)}, bf16[128,16384]{1,0:T(8,128)(2,1)S(1)}, u32[]{:S(2)}, u32[]{:S(2)}) collective-permute-start(bf16[128,16384]{1,0:T(8,128)(2,1)S(1)} %bitcast.53), channel_id=1, source_target_pairs={{24,0},{0,8},{8,16},{16,24},{25,1},{1,9},{9,17},{17,25},{26,2},{2,... | collective-permute-start | bytes 12582920 | tf_op jit(solution)/shard_map/ppermute | solution.py:13
where the time goes:
time: 288 us; the launch traced here: 287 us
  blocking collectives  131 us (45%)
  waiting for transfers between devices  91.3 us (32%)
  local copies, waits for them, and re-layouts  42 us (15%)
  matrix products  12.6 us (4%)
  other arithmetic  6.85 us (2%)
    all_to_all x1, blocking collectives, spread_rows(): lax.all_to_all(flat_buffer, ('cp', 'tp'), split_axis=0, concat_axis=0, ti...  97.9 us
    ppermute x1, waiting for transfers between devices, shifted(): return lax.ppermute(block, axis, route)  91.3 us
    all_gather x1, blocking collectives, body(): key_piece = lax.all_gather(keys, 'cp', axis=0, tiled=True)  17.4 us
    convert_element_type x1, local copies, waits for them, and re-layouts, body(): weights.astype(jnp.bfloat16).reshape(stat_shape + (block, 2 * block_len))  17.2 us
    all_gather x1, blocking collectives, body(): value_piece = lax.all_gather(values, 'cp', axis=0, tiled=True)  16.2 us
    unnamed x11, local copies, waits for them, and re-layouts  9.69 us
    reshape x1, local copies, waits for them, and re-layouts, spread_rows(): moved.reshape(cycle_size, split_size, capacity, width)  6.38 us
    reduce_sum x1, other arithmetic, body(): running_total = running_total * carry_factor + jnp.sum(weights, axis=4)  6.22 us
  transfers between devices with their start and end apart: 1, of which 1 were waited for; matrix products, arithmetic and copies ran while one was open for 0% of the time, Pallas kernels for 0%

commit v1 on v0

--- a/solution.py
+++ b/solution.py
@@ -76,7 +76,12 @@
     )
     state = start_state
     key_piece = lax.all_gather(keys, "cp", axis=0, tiled=True)
-    value_piece = lax.all_gather(values, "cp", axis=0, tiled=True)
+    ring = [values]
+    for hop in range(3):
+        ring.append(lax.ppermute(ring[-1], "cp", [(dev, (dev + 1) % 4) for dev in range(4)]))
+    value_piece = jnp.roll(
+        jnp.concatenate(ring[::-1], axis=0), (lax.axis_index("cp") + 1) * ring[0].shape[0], axis=0
+    )
     shard_count = key_piece.shape[0] // row_count
     first_shard = jnp.int32(0) // row_count
     for base in range(0, shard_count, 4):

time: 288 us -> 268 us (0.931)
  blocking collectives: 131 us -> 112 us
  local copies, waits for them, and re-layouts: 42 us -> 24.7 us
  waiting for transfers between devices: 91.3 us -> 104 us
  starting transfers between devices: 1.55 us -> 5.15 us
    convert_element_type x1 -> x0, local copies, waits for them, and re-layouts: 17.2 us -> none  [body(): weights.astype(jnp.bfloat16).reshape(stat_shape + (block, 2 * block_len))]
    all_gather x1 -> x0, blocking collectives: 16.2 us -> none  [body(): value_piece = lax.all_gather(values, 'cp', axis=0, tiled=True)]
    ppermute x0 -> x3, waiting for transfers between devices: none -> 13 us  [body(): lax.ppermute(ring[-1], 'cp', [(dev, (dev + 1) % 4) for dev in range(4)])]
    ppermute x0 -> x3, starting transfers between devices: none -> 3.6 us  [body(): lax.ppermute(ring[-1], 'cp', [(dev, (dev + 1) % 4) for dev in range(4)])]
    unnamed x11 -> x16, local copies, waits for them, and re-layouts: 9.69 us -> 9.08 us
  transfers between devices with their start and end apart: 1 -> 4, of which waited for: 1 -> 3; matrix products, arithmetic and copies ran while one was open for 0% -> 7% of each run, Pallas kernels for 0% -> 0%
where the time goes in v1:
time: 268 us
  blocking collectives  112 us (42%)
  waiting for transfers between devices  104 us (39%)
  local copies, waits for them, and re-layouts  24.7 us (9%)
  matrix products  13.6 us (5%)
  other arithmetic  6.84 us (3%)
  starting transfers between devices  5.15 us (2%)
    all_to_all x1, blocking collectives, spread_rows(): lax.all_to_all(flat_buffer, ('cp', 'tp'), split_axis=0, concat_axis=0, ti...  96.5 us
    ppermute x1, waiting for transfers between devices, shifted(): return lax.ppermute(block, axis, route)  91.3 us
    all_gather x1, blocking collectives, body(): key_piece = lax.all_gather(keys, 'cp', axis=0, tiled=True)  15.3 us
    ppermute x3, waiting for transfers between devices, body(): lax.ppermute(ring[-1], 'cp', [(dev, (dev + 1) % 4) for dev in range(4)])  13 us
    unnamed x16, local copies, waits for them, and re-layouts  9.08 us
    dot_general x1, matrix products, body(): jnp.einsum('sqgrnk,nskgd->sqgrd', shaped, value_block, preferred_element_...  6.76 us
    reshape x1, local copies, waits for them, and re-layouts, spread_rows(): moved.reshape(cycle_size, split_size, capacity, width)  6.38 us
    reduce_sum x1, other arithmetic, body(): running_total = running_total * carry_factor + jnp.sum(weights, axis=4)  6.2 us
  transfers between devices with their start and end apart: 4, of which 3 were waited for; matrix products, arithmetic and copies ran while one was open for 7% of the time, Pallas kernels for 0%

profile of v1, /device:TPU:0, one launch (start us, length us, event | category | flops | bytes accessed | tf_op | source)
XLA Modules:
  0.0 268.1 jit_solution(13775427035968339375)
XLA Ops:
  0.0 0.0 copy-start
  0.0 0.0 copy-start.2
  0.0 3.0 %collective-permute-start = (bf16[128,512]{1,0:T(8,128)(2,1)}, bf16[128,512]{1,0:T(8,128)(2,1)S(1)}, u32[]{:S(2)}, u32[]{:S(2)}) collective-permute-start(bf16[128,512]{1,0:T(8,128)(2,1)} %param.8), channel_id=1, source_target_pairs={{0,2},{2,4},{4,6},{6,0},{1,3},{3,5},{5,7},{7,1},{8,10},{10,12},{12... | collective-permute-start | bytes 393224 | tf_op jit(solution)/shard_map/ppermute | solution.py:81
  3.0 0.7 fusion.18
  3.7 1.3 dynamic_slice.22
  6.3 0.6 gather_fusion
  6.9 0.9 dynamic-slice_reduce_fusion
  7.8 0.1 add_bitcast_fusion
  7.9 0.1 iota_add_fusion
  8.0 0.1 pad_add_fusion
  8.0 0.1 broadcast_compare_fusion
  8.2 0.1 broadcast_compare_fusion.1
  8.2 2.2 copy.28
  10.4 0.0 copy-done.2
  10.4 15.3 %all_gather.3 = bf16[512,512]{1,0:T(8,128)(2,1)S(1)} all-gather(bf16[128,512]{1,0:T(8,128)(2,1)S(1)} %copy-done.2), channel_id=1, replica_groups=mesh['pp'=4,'cp'=4,'tp'=2] {'cp'}, dimensions={0}, use_global_device_ids=true | all-gather | bytes 655360 | tf_op jit(solution)/shard_map/all_gather | solution.py:78
  25.8 0.1 reshape.234
  25.9 0.1 broadcast_and_fusion
  26.0 5.5 %fusion = (f32[2,64,4,16]{1,3,2,0:T(8,128)S(1)}, f32[2,4,4,64,64,16]{4,3,5,2,1,0:T(8,128)S(1)}) fusion(pred[2,64,4,64]{1,3,2,0:T(8,128)(4,1)S(1)} %broadcast_and_fusion, bf16[2,64,4,16,128,1]{4,3,2,1,0,5:T(8,128)(2,1)S(1)} %bitcast.51, bf16[4,2,64,4,128,1]{4,3,2,1,0,5:T(4,128)(2,1)S(1)} %bitcast.53), kind=kOutput, calls=%fused_computation.3 | convolution fusion | flops 543154176 | bytes 11075584 | tf_op jit(solution)/shard_map/sqgrd,nskgd->sqgrnk/dot_general | solution.py:104
  31.6 0.0 copy-start.1
  31.6 6.2 %fusion.3 = (f32[2,64,4,16]{1,3,2,0:T(8,128)S(1)}, bf16[2,64,4,16,4,64]{1,5,3,4,2,0:T(8,128)(2,1)}) fusion(f32[2,4,4,64,64,16]{4,3,5,2,1,0:T(8,128)S(1)} %get-tuple-element.12, f32[2,64,4,16]{1,3,2,0:T(8,128)S(1)} %broadcast_maximum_fusion, pred[2,64,4,64]{1,3,2,0:T(8,128)(4,1)S(1)} %broadcast_and_fusion), kind=kLoop, calls=%fused_computation.6 | loop fusion | flops 10477568 | bytes 12681216 | tf_op jit(solution)/shard_map/reduce_sum | solution.py:113
  37.8 0.0 copy-done
  37.8 0.1 fusion.13
  38.0 0.0 collective-permute-done
  38.0 0.6 collective-permute-start.1
  38.6 6.2 %collective-permute-done.1 = bf16[128,512]{1,0:T(8,128)(2,1)S(1)} collective-permute-done((bf16[128,512]{1,0:T(8,128)(2,1)S(1)}, bf16[128,512]{1,0:T(8,128)(2,1)S(1)}, u32[]{:S(2)}, u32[]{:S(2)}) %collective-permute-start.1) | collective-permute-done | bytes 131104 | tf_op jit(solution)/shard_map/ppermute | solution.py:81
  44.9 0.0 collective-permute-start.2
  44.9 6.7 %collective-permute-done.2 = bf16[128,512]{1,0:T(8,128)(2,1)S(1)} collective-permute-done((bf16[128,512]{1,0:T(8,128)(2,1)S(1)}, bf16[128,512]{1,0:T(8,128)(2,1)S(1)}, u32[]{:S(2)}, u32[]{:S(2)}) %collective-permute-start.2) | collective-permute-done | bytes 131104 | tf_op jit(solution)/shard_map/ppermute | solution.py:81
  51.7 0.0 copy-done.1
  51.8 0.1 reshape.236
  52.0 6.8 %fusion.8 = bf16[2,64,4,16,128]{4,1,3,2,0:T(8,128)(2,1)S(1)} fusion(bf16[2,64,4,16,4,64]{1,5,3,4,2,0:T(8,128)(2,1)} %get-tuple-element.6, f32[2,64,4,16]{1,3,2,0:T(8,128)S(1)} %get-tuple-element.8, f32[2,64,4,16]{1,3,2,0:T(8,128)S(1)} %get-tuple-element.7, bf16[4,2,64,4,128,1]{4,3,2,1,0,5:T(4,128)(2,1)S(1)} %bitcast.55), kind=kOutput, calls=%fused_computation.13 | convolution fusion | flops 540016640 | bytes 6881280 | tf_op jit(solution)/shard_map/sqgrnk,nskgd->sqgrd/dot_general | solution.py:115
  58.7 2.7 copy.14
  61.4 2.8 %reshape.237 = bf16[128,8192]{1,0:T(8,128)(2,1)S(1)} reshape(bf16[2,64,4,16,128]{4,3,2,1,0:T(8,128)(2,1)} %copy.14) | data formatting | bytes 4194304 | tf_op jit(solution)/shard_map/reshape | solution.py:119
  64.2 1.2 convolution_convert_fusion
  65.5 96.5 %all_to_all.5 = bf16[8,32,8192]{2,1,0:T(8,128)(2,1)S(1)} all-to-all(bf16[8,32,8192]{2,1,0:T(8,128)(2,1)S(1)} %bitcast.48), channel_id=1, replica_groups=mesh['pp'=4,'cp'=4,'tp'=2] {'cp','tp'}, dimensions={0} | all-to-all | bytes 8388608 | tf_op jit(solution)/shard_map/all_to_all | solution.py:40
  162.0 6.4 %copy.15 = bf16[4,2,32,8192]{3,1,2,0:T(2,128)(2,1)} copy(bf16[4,2,32,8192]{3,2,1,0:T(8,128)(2,1)S(1)} %bitcast.49) | data formatting | bytes 8388608 | tf_op jit(solution)/shard_map/reshape | solution.py:41
  168.4 4.8 %copy.29 = bf16[16,8,2,8192]{3,1,2,0:T(8,128)(2,1)S(1)} copy(bf16[16,8,2,8192]{3,2,1,0:T(2,128)(2,1)} %bitcast.50) | data formatting | bytes 8388608
  173.2 1.5 collective-permute-start.3
  174.7 91.3 %collective-permute-done.3 = bf16[128,16384]{1,0:T(8,128)(2,1)S(1)} collective-permute-done((bf16[128,16384]{1,0:T(8,128)(2,1)S(1)}, bf16[128,16384]{1,0:T(8,128)(2,1)S(1)}, u32[]{:S(2)}, u32[]{:S(2)}) %collective-permute-start.3) | collective-permute-done | bytes 4194336 | tf_op jit(solution)/shard_map/ppermute | solution.py:13
  266.1 2.0 copy.54
  (20 shorter events, 0.2 us)
Async XLA Ops:
  0.0 37.8 %copy-start = (s32[4,128,1]{1,2,0:T(1,128)S(1)}, s32[4,128,1]{1,2,0:T(1,128)}, u32[]{:S(2)}) copy-start(s32[4,128,1]{1,2,0:T(1,128)} %param.11) | copy-start | bytes 6148
  0.0 10.4 %copy-start.2 = (bf16[128,512]{1,0:T(8,128)(2,1)S(1)}, bf16[128,512]{1,0:T(8,128)(2,1)}, u32[]{:S(2)}) copy-start(bf16[128,512]{1,0:T(8,128)(2,1)} %param.7) | copy-start | bytes 393220
  0.0 38.0 %collective-permute-start = (bf16[128,512]{1,0:T(8,128)(2,1)}, bf16[128,512]{1,0:T(8,128)(2,1)S(1)}, u32[]{:S(2)}, u32[]{:S(2)}) collective-permute-start(bf16[128,512]{1,0:T(8,128)(2,1)} %param.8), channel_id=1, source_target_pairs={{0,2},{2,4},{4,6},{6,0},{1,3},{3,5},{5,7},{7,1},{8,10},{10,12},{12... | collective-permute-start | bytes 393224 | tf_op jit(solution)/shard_map/ppermute | solution.py:81
  31.6 20.1 %copy-start.1 = (bf16[128,512]{1,0:T(8,128)(2,1)S(1)}, bf16[128,512]{1,0:T(8,128)(2,1)}, u32[]{:S(2)}) copy-start(bf16[128,512]{1,0:T(8,128)(2,1)} %param.8) | copy-start | bytes 393220
  38.0 6.8 %collective-permute-start.1 = (bf16[128,512]{1,0:T(8,128)(2,1)S(1)}, bf16[128,512]{1,0:T(8,128)(2,1)S(1)}, u32[]{:S(2)}, u32[]{:S(2)}) collective-permute-start(bf16[128,512]{1,0:T(8,128)(2,1)S(1)} %collective-permute-done), channel_id=1, source_target_pairs={{0,2},{2,4},{4,6},{6,0},{1,3},{3,5},{5,7},{7,1},{8,10},{10,12},{12... | collective-permute-start | bytes 393224 | tf_op jit(solution)/shard_map/ppermute | solution.py:81
  44.9 6.8 %collective-permute-start.2 = (bf16[128,512]{1,0:T(8,128)(2,1)S(1)}, bf16[128,512]{1,0:T(8,128)(2,1)S(1)}, u32[]{:S(2)}, u32[]{:S(2)}) collective-permute-start(bf16[128,512]{1,0:T(8,128)(2,1)S(1)} %collective-permute-done.1), channel_id=1, source_target_pairs={{0,2},{2,4},{4,6},{6,0},{1,3},{3,5},{5,7},{7,1},{8,10},{10,12},{12... | collective-permute-start | bytes 393224 | tf_op jit(solution)/shard_map/ppermute | solution.py:81
  173.2 92.9 %collective-permute-start.3 = (bf16[128,16384]{1,0:T(8,128)(2,1)S(1)}, bf16[128,16384]{1,0:T(8,128)(2,1)S(1)}, u32[]{:S(2)}, u32[]{:S(2)}) collective-permute-start(bf16[128,16384]{1,0:T(8,128)(2,1)S(1)} %bitcast.52), channel_id=1, source_target_pairs={{24,0},{0,8},{8,16},{16,24},{25,1},{1,9},{9,17},{17,25},{26,2},{2,... | collective-permute-start | bytes 12582920 | tf_op jit(solution)/shard_map/ppermute | solution.py:13
